TPU v7x, 256 devices: a whole 4x4x8 slice. The times are simulated.
256 devices in a mesh: row: 16 (over y, x), col: 16 (over z, core).
Axes of the slice: x: 4, y: 4, z: 8, core: 2. Of those that a mesh axis runs over, the one named last changes fastest.
Arguments:
- trail_grad: float32 [16384, 16384], P('row', 'col'), may hold values from -20 to 20, as said below
- factor_rows: float32 [16384, 768], P('col', 'row'), may hold values from -0.046875 to 0.046875
- factor_top: float32 [768, 768], replicated, may hold values from -1 to 2, as said below
- rows_grad: float32 [16384, 768], P(('row', 'col')), may hold values from -6 to 6
- top_grad: float32 [768, 768], replicated, may hold values from -6 to 6, as said below
Outputs:
- rows_adjoint: float32 [16384, 768], P(('row', 'col'))
- top_adjoint: float32 [768, 768], replicated
Inputs may be any that keep to these rules, and one draw needn't show every extreme that they name: trail_grad is symmetric once both of its orders are reverted. factor_top is lower triangular with its diagonal between 1 and 2. top_grad is lower triangular.
All inputs are finite; a program needn't handle non-finite values.
Results may differ from a plain program's by a relative error of at most 0.0001.
Values sent between devices are 32-bit elements; how exact they have to be, the bound alone decides.
A program may use at most 64 MiB of HBM per device.

v0:
```python
import jax
import jax.numpy as jnp
from jax import lax
from jax.sharding import PartitionSpec as P

NB = 256
NP = 3
CB = 128


exact_dots = lax.Precision.HIGHEST


def product(left, right):
    return jnp.dot(left, right, precision=exact_dots, preferred_element_type=jnp.float32)


def column_products(left, right):
    return jnp.einsum(
        "ia,ib->ab", left, right, precision=exact_dots, preferred_element_type=jnp.float32
    )


def halve_diagonal(matrix):
    order = matrix.shape[0]
    row_ids = lax.broadcasted_iota(jnp.int32, (order, order), 0)
    col_ids = lax.broadcasted_iota(jnp.int32, (order, order), 1)
    return jnp.where(row_ids > col_ids, matrix, jnp.where(row_ids == col_ids, 0.5 * matrix, 0.0))


def cholesky_adjoint(factor, inverse, gradient):
    inner = halve_diagonal(product(factor.T, gradient))
    middle = product(product(inverse.T, inner), inverse)
    return halve_diagonal(middle + middle.T)


def per_device(trail_grad, factor_rows, factor_top, rows_grad, top_grad):
    row_owner = lax.axis_index("row")
    col_owner = lax.axis_index("col")
    row_owners = lax.axis_size("row")
    col_owners = lax.axis_size("col")
    owned_rows = trail_grad.shape[0]
    tiles_row = owned_rows // CB
    tiles_col = trail_grad.shape[1] // CB
    panel_width = NP * NB
    piece_rows = rows_grad.shape[0]
    panels = lax.all_gather(factor_rows, "row", axis=1, tiled=True)
    global_rows = (
        lax.broadcasted_iota(jnp.int32, (tiles_row, tiles_col), 0) * row_owners + row_owner
    )
    global_cols = (
        lax.broadcasted_iota(jnp.int32, (tiles_row, tiles_col), 1) * col_owners + col_owner
    )
    intersection = (global_rows == global_cols).astype(jnp.float32)
    aligned_rows = jnp.einsum(
        "kq,qtw->ktw",
        intersection,
        panels.reshape(tiles_col, CB, panel_width),
        precision=exact_dots,
        preferred_element_type=jnp.float32,
    ).reshape(owned_rows, panel_width)
    cross_factor = lax.psum_scatter(aligned_rows, "col", scatter_dimension=0, tiled=True)
    row_index = lax.broadcasted_iota(jnp.int32, (panel_width, NB), 0)
    identity = jnp.eye(NB, dtype=jnp.float32)
    adj_here = jnp.zeros((piece_rows, panel_width), jnp.float32)
    adj_top = jnp.zeros((panel_width, panel_width), jnp.float32)
    cross_adjoints = [None] * NP
    for which_panel in reversed(range(NP)):
        col_start = which_panel * NB
        col_end = col_start + NB
        below_diag = jnp.where(row_index >= col_end, factor_top[:, col_start:col_end], 0.0)
        diag_block = factor_top[col_start:col_end, col_start:col_end]
        inverse = jax.scipy.linalg.solve_triangular(diag_block, identity, lower=True)
        partial_rows = product(trail_grad, panels[:, col_start:col_end])
        summed_rows = lax.psum_scatter(partial_rows, "col", scatter_dimension=0, tiled=True)
        rows_cbar = (
            rows_grad[:, col_start:col_end] - 2.0 * summed_rows - product(adj_here, below_diag)
        )
        later_blocks = []
        if which_panel < NP - 1:
            cross_terms = jnp.stack(
                [
                    column_products(cross_adjoints[later_panel], cross_factor[:, col_start:col_end])
                    for later_panel in range(which_panel + 1, NP)
                ]
            )
            cross_summed = lax.psum(cross_terms, ("row", "col"))
            later_blocks = [
                cross_summed[later_panel - which_panel - 1]
                for later_panel in range(which_panel + 1, NP)
            ]
        if later_blocks:
            cross_part = jnp.concatenate([jnp.zeros((col_end, NB), jnp.float32)] + later_blocks, 0)
        else:
            cross_part = jnp.zeros((panel_width, NB), jnp.float32)
        top_masked = jnp.where(row_index >= col_end, top_grad[:, col_start:col_end], 0.0)
        top_cbar = top_masked - (product(adj_top + adj_top.T, below_diag) + cross_part)
        rows_adj = product(rows_cbar, inverse)
        top_adj = product(top_cbar, inverse)
        diag_sum = lax.psum(
            column_products(rows_adj, cross_factor[:, col_start:col_end]), ("row", "col")
        )
        diag_grad = jnp.tril(
            top_grad[col_start:col_end, col_start:col_end]
            - product(top_adj.T, below_diag)
            - diag_sum
        )
        diag_adjoint = cholesky_adjoint(diag_block, inverse, diag_grad)
        cross_adjoints[which_panel] = rows_adj
        adj_here = adj_here.at[:, col_start:col_end].set(rows_adj)
        adj_top = adj_top.at[:, col_start:col_end].set(
            top_adj.at[col_start:col_end].set(diag_adjoint)
        )
    return (adj_here, adj_top)


def solution(mesh):
    placed = (P("row", "col"), P("col", "row"), P(), P(("row", "col"), None), P())
    return jax.shard_map(
        per_device,
        mesh=mesh,
        in_specs=placed,
        out_specs=(P(("row", "col"), None), P()),
        check_vma=False,
    )
```

profile of v0, /device:TPU:1, one launch (start us, length us, event | category | flops | bytes accessed | tf_op | source)
XLA Modules:
  0.0 638.1 jit_solution(12279739426921874140)
XLA Ops:
  7.9 58.4 %all-gather.2.cloned.1.call-done = f32[1024,768]{0,1:T(8,128)} async-done(((f32[1024,48]{0,1:T(8,128)}), f32[1024,768]{0,1:T(8,128)}) %all-gather.2.cloned.1.call-update) | async-done | bytes 3145744 | tf_op jit(solution)/shard_map/all_gather | solution.py:47
  66.4 7.1 %fusion.16 = f32[1024,256]{1,0:T(8,128)} fusion(f32[1024,1024]{1,0:T(8,128)} %param.25, f32[1024,768]{0,1:T(8,128)} %all-gather.2.cloned.1.call-done), kind=kOutput, calls=%fused_computation.40 | convolution fusion | flops 3221225472 | bytes 6291456 | tf_op jit(solution)/shard_map/dot_general | solution.py:15
  73.5 6.6 %fusion.14 = f32[1024,256]{1,0:T(8,128)} fusion(f32[1024,1024]{1,0:T(8,128)} %param.25, f32[1024,768]{0,1:T(8,128)S(1)} %copy-done.2), kind=kOutput, calls=%fused_computation.38 | convolution fusion | flops 3221225472 | bytes 6291456 | tf_op jit(solution)/shard_map/dot_general | solution.py:15
  80.2 6.6 %fusion.12 = f32[1024,256]{1,0:T(8,128)} fusion(f32[1024,1024]{1,0:T(8,128)} %param.25, f32[1024,768]{0,1:T(8,128)S(1)} %copy-done.2), kind=kOutput, calls=%fused_computation.36 | convolution fusion | flops 3221225472 | bytes 6291456 | tf_op jit(solution)/shard_map/dot_general | solution.py:15
  87.1 2.4 copy.50
  89.5 3.3 fusion
  92.9 2.6 copy.52
  95.5 1.6 copy-done
  97.3 3.8 while.15
  97.9 1.3 bitcast_dynamic-update-slice_fusion.6
  99.8 1.3 bitcast_dynamic-update-slice_fusion.6
  101.1 19.7 %custom-call.5 = f32[2,128,128]{1,2,0:T(8,128)S(1)} custom-call(f32[2,128,128]{2,1,0:T(8,128)S(1)} %get-tuple-element.131), custom_call_target="InvertDiagBlocksLowerTriangular" | custom-call | tf_op jit(solution)/shard_map/jit(_solve_triangular)/triangular_solve | solution.py:73
  120.8 3.8 while.16
  121.4 1.3 bitcast_dynamic-update-slice_fusion.7
  123.3 1.3 bitcast_dynamic-update-slice_fusion.7
  124.6 20.3 %custom-call.6 = f32[2,128,128]{1,2,0:T(8,128)} custom-call(f32[2,128,128]{2,1,0:T(8,128)S(1)} %get-tuple-element.132), custom_call_target="InvertDiagBlocksLowerTriangular" | custom-call | tf_op jit(solution)/shard_map/jit(_solve_triangular)/triangular_solve | solution.py:73
  144.9 3.7 while.17
  145.5 1.2 bitcast_dynamic-update-slice_fusion.8
  147.4 1.2 bitcast_dynamic-update-slice_fusion.8
  148.6 20.3 %custom-call.7 = f32[2,128,128]{1,2,0:T(8,128)} custom-call(f32[2,128,128]{2,1,0:T(8,128)S(1)} %get-tuple-element.133), custom_call_target="InvertDiagBlocksLowerTriangular" | custom-call | tf_op jit(solution)/shard_map/jit(_solve_triangular)/triangular_solve | solution.py:73
  171.5 1.2 fusion.80
  173.9 1.2 fusion.91
  176.0 1.6 convolution_subtract_fusion.8
  177.8 10.7 %reduce-scatter.7.cloned.1.call-done = f32[64,256]{1,0:T(8,128)} async-done(((f32[1024,256]{1,0:T(8,128)}), f32[64,256]{1,0:T(8,128)}) %reduce-scatter.7.cloned.1.call-update) | async-done | bytes 65552 | tf_op jit(solution)/shard_map/reduce_scatter | solution.py:75
  188.5 1.5 convolution_subtract_fusion.7
  190.9 56.7 %reduce-scatter.9.cloned.1.call-done = f32[64,256]{1,0:T(8,128)} async-done(((f32[1024,256]{1,0:T(8,128)}), f32[64,256]{1,0:T(8,128)}) %reduce-scatter.9.cloned.1.call-update) | async-done | bytes 65552 | tf_op jit(solution)/shard_map/reduce_scatter | solution.py:75
  247.6 1.5 convolution_subtract_fusion.6
  250.0 59.9 %reduce-scatter.11.cloned.1.call-done = f32[64,768]{1,0:T(8,128)} async-done(((f32[1024,768]{1,0:T(8,128)}), f32[64,768]{1,0:T(8,128)}) %reduce-scatter.11.cloned.1.call-update) | async-done | bytes 196624 | tf_op jit(solution)/shard_map/reduce_scatter | solution.py:62
  309.8 1.3 convolution_bitcast_fusion.3
  311.2 1.3 convolution_bitcast_fusion.4
  313.3 1.9 fusion.85
  315.2 2.0 fusion.96
  319.6 2.0 fusion.22
  321.6 261.7 %all-reduce.6.cloned.1.call-done = (f32[256,256]{1,0:T(8,128)}, f32[256,256]{1,0:T(8,128)}, f32[256,256]{1,0:T(8,128)}, f32[2,256,256]{2,1,0:T(8,128)}, f32[256,256]{1,0:T(8,128)}) async-done(((f32[256,256]{1,0:T(8,128)}, f32[256,256]{1,0:T(8,128)}, f32[256,256]{1,0:T(8,128)}, f32[2,256,256]{2,1,0:T(8,128)}, f32[256,256]{1,0:T(8,128)}), (f32[256,256]{1,0:T(8,128)}, f32[256,256]{1,0:T(8,128)}, ...) | async-done | bytes 1572880 | tf_op jit(solution)/shard_map/psum | solution.py:100
  583.4 2.6 fusion.9
  587.8 1.1 copy.55
  588.9 1.5 pad_bitcast_fusion
  590.6 1.6 copy-done.1
  592.1 3.5 fusion.5
  596.4 2.5 fusion.10
  603.4 1.6 broadcast_select_fusion
  604.9 1.4 copy.58
  606.4 2.0 copy.59
  609.4 6.2 fusion.4
  617.6 2.8 fusion.11
  620.4 1.6 convolution_bitcast_fusion
  623.7 1.8 copy.61
  629.1 2.0 copy.64
  (108 shorter events, 30.1 us)
Async XLA Ops:
  7.2 59.2 %all-gather.2.cloned.1.call-start = ((), (), s32[]{:S(2)}) async-start(), calls=%async_computation.4 | async-start | bytes 3342336 | tf_op jit(solution)/shard_map/all_gather | solution.py:47
  7.9 168.1 %reduce-scatter.5.cloned.1.call-start = ((), (), s32[]{:S(2)}) async-start(), calls=%async_computation.5 | async-start | bytes 1114112 | tf_op jit(solution)/shard_map/reduce_scatter | solution.py:75
  66.4 7.1 %copy-start.2 = (f32[1024,768]{0,1:T(8,128)S(1)}, f32[1024,768]{0,1:T(8,128)}, u32[]{:S(2)}) copy-start(f32[1024,768]{0,1:T(8,128)} %all-gather.2.cloned.1.call-done) | copy-start | bytes 9437188
  73.5 115.0 %reduce-scatter.7.cloned.1.call-start = ((), (), s32[]{:S(2)}) async-start(), calls=%async_computation.6 | async-start | bytes 1114112 | tf_op jit(solution)/shard_map/reduce_scatter | solution.py:75
  80.2 167.4 %reduce-scatter.9.cloned.1.call-start = ((), (), s32[]{:S(2)}) async-start(), calls=%async_computation.7 | async-start | bytes 1114112 | tf_op jit(solution)/shard_map/reduce_scatter | solution.py:75
  86.9 223.0 %reduce-scatter.11.cloned.1.call-start = ((), (), s32[]{:S(2)}) async-start(), calls=%async_computation.8 | async-start | bytes 3342336 | tf_op jit(solution)/shard_map/reduce_scatter | solution.py:62
  95.5 1.7 copy-start
  95.5 487.9 %all-reduce.6.cloned.1.call-start = ((), (), s32[]{:S(2)}) async-start(), calls=%async_computation.9 | async-start | bytes 3145728 | tf_op jit(solution)/shard_map/psum | solution.py:100
  124.6 46.0 %copy-start.11 = (f32[256,256]{1,0:T(8,128)}, f32[256,256]{1,0:T(8,128)S(1)}, u32[]{:S(2)}) copy-start(f32[256,256]{1,0:T(8,128)S(1)} %get-tuple-element.347) | copy-start | bytes 786436
  168.9 6.1 copy-start.16
  171.5 18.5 %copy-start.8 = (f32[128,256]{1,0:T(8,128)}, f32[128,256]{1,0:T(8,128)S(1)}, u32[]{:S(2)}) copy-start(f32[128,256]{1,0:T(8,128)S(1)} %fusion.93) | copy-start | bytes 393220
  175.0 74.1 %copy-start.6 = (f32[128,256]{1,0:T(8,128)}, f32[128,256]{1,0:T(8,128)S(1)}, u32[]{:S(2)}) copy-start(f32[128,256]{1,0:T(8,128)S(1)} %fusion.91) | copy-start | bytes 393220
  175.9 74.0 %copy-start.4 = (f32[128,256]{1,0:T(8,128)}, f32[128,256]{1,0:T(8,128)S(1)}, u32[]{:S(2)}) copy-start(f32[128,256]{1,0:T(8,128)S(1)} %fusion.89) | copy-start | bytes 393220
  250.0 69.5 %copy-start.12 = (f32[64,768]{1,0:T(8,128)}, f32[64,768]{1,0:T(8,128)S(1)}, u32[]{:S(2)}) copy-start(f32[64,768]{1,0:T(8,128)S(1)} %get-tuple-element.184) | copy-start | bytes 589828
  309.8 7.3 %copy-start.13 = (f32[64,768]{1,0:T(8,128)S(1)}, f32[64,768]{1,0:T(8,128)}, u32[]{:S(2)}) copy-start(f32[64,768]{1,0:T(8,128)} %reduce-scatter.11.cloned.1.call-done) | copy-start | bytes 589828
  583.4 3.2 copy-start.9
  588.9 1.5 copy-start.3
  588.9 1.6 copy-start.15
  590.4 1.7 copy-start.1
  592.1 3.5 copy-start.7
  592.1 4.3 copy-start.14
  609.4 6.2 copy-start.5
  620.4 7.0 %copy-start.10 = (f32[768,256]{0,1:T(8,128)S(1)}, f32[768,256]{0,1:T(8,128)}, u32[]{:S(2)}) copy-start(f32[768,256]{0,1:T(8,128)} %copy.62) | copy-start | bytes 2359300
Sparse Core Ops, SparseCore 0:
  10.4 55.9 all-gather.1
  73.6 55.2 reduce-scatter.4
  131.4 57.0 reduce-scatter.6
  190.9 56.6 reduce-scatter.8
  250.0 59.8 reduce-scatter.10
  319.6 263.7 all-reduce.5
where the time goes:
time: 648 us; the launch traced here: 638 us
  waiting for transfers between devices  448 us (69%)
  matrix products  72.5 us (11%)
  other arithmetic  67.5 us (10%)
  local copies, waits for them, and re-layouts  34.5 us (5%)
  between operations  14.9 us (2%)
    psum x1, waiting for transfers between devices, per_device(): lax.psum(column_products(rows_adj, cross_factor[:, col_start:col_end]), (...  262 us
    reduce_scatter x3, waiting for transfers between devices, per_device(): lax.psum_scatter(partial_rows, 'col', scatter_dimension=0, tiled=True)  67.4 us
    another operation x5, other arithmetic, per_device(): jax.scipy.linalg.solve_triangular(diag_block, identity, lower=True)  60.3 us
    reduce_scatter x1, waiting for transfers between devices, per_device(): lax.psum_scatter(aligned_rows, 'col', scatter_dimension=0, tiled=True)  59.9 us
    all_gather x1, waiting for transfers between devices, per_device(): panels = lax.all_gather(factor_rows, 'row', axis=1, tiled=True)  58.4 us
    dot_general x26, matrix products, product(): jnp.dot(left, right, precision=exact_dots, preferred_element_type=jnp.flo...  55.2 us
  transfers between devices with their start and end apart: 6, of which 5 were waited for; matrix products, arithmetic and copies ran while one was open for 17% of the time, Pallas kernels for 0%

commit v1 on v0

v1 whole, which is shorter than its diff:
```python
import jax
import jax.numpy as jnp
from jax import lax
from jax.experimental import pallas as pl
from jax.experimental.pallas import tpu as pltpu
from jax.sharding import PartitionSpec as P

MESH = pl.DeviceIdType.MESH
F32, BF16 = jnp.float32, jnp.bfloat16
HIGHEST = lax.Precision.HIGHEST
NX, NY, NZ = 4, 4, 8
BLOCK, HALF, WIDTH = 256, 128, 768
CHUNK, PIECE = 48, 24
GROUP, SUB = 192, 96
OFFSETS = (0, 768, 1280)
SEMAPHORES = 200


def contract(left, right, dims, precision=None):
    return lax.dot_general(left, right, (dims, ((), ())), precision=precision, preferred_element_type=F32)


def split(value):
    high = value.astype(BF16)
    return high, (value - high.astype(F32)).astype(BF16)


def dot3(left, right, dims=((1,), (0,))):
    left_high, left_low = split(left)
    right_high, right_low = split(right)
    return (
        contract(left_low, right_high, dims)
        + contract(left_high, right_low, dims)
        + contract(left_high, right_high, dims)
    )


def dot6(left, right):
    return contract(left, right, ((1,), (0,)), HIGHEST)


def iota(shape, dim):
    return lax.broadcasted_iota(jnp.int32, shape, dim)


def aligned(index, unit):
    return pl.multiple_of(index * unit, unit)


def kernel(trail, factor, lower, grad, top, out_rows, out_top, strail, s_high, s_low, f_all, zt, cx, zc, r_left, r_right, low, topv,
           inv, inv_t, cmat, mmat, xmat, gbuf, p_hat, p_rows, f_own, wst, r_a1, r_a2, a1, a2, r_b1, r_b2, b1, b2, r_c1, r_c2, c1, c2,
           wfull, local_sem, send_sem, recv_sem):
    row, col = lax.axis_index("row"), lax.axis_index("col")
    y, x = lax.div(row, NX), lax.rem(row, NX)
    z, k = lax.div(col, 2), lax.rem(col, 2)
    other = 1 - k

    def at_x(d):
        return (y * NX + lax.rem(x + d + NX, NX), col)

    def at_y(d):
        return (lax.rem(y + d + NY, NY) * NX + x, col)

    def at_z(d):
        return (row, lax.rem(z + d + NZ, NZ) * 2 + k)

    partner = (row, z * 2 + other)
    count = [0]
    pending = []

    def push(src, dst, device):
        slot = count[0]
        count[0] += 1
        copy = pltpu.make_async_remote_copy(
            src_ref=src, dst_ref=dst, send_sem=send_sem.at[slot], recv_sem=recv_sem.at[slot], device_id=device, device_id_type=MESH
        )
        copy.start()
        pending.append(copy)
        return copy

    local = [
        pltpu.make_async_copy(factor, f_all.at[pl.ds(aligned(row, CHUNK), CHUNK)], local_sem.at[0]),
        pltpu.make_async_copy(grad, gbuf.at[pl.ds(aligned(k, 64), 64)], local_sem.at[1]),
        pltpu.make_async_copy(trail, strail, local_sem.at[2]),
        pltpu.make_async_copy(lower, low, local_sem.at[3]),
        pltpu.make_async_copy(top, topv, local_sem.at[4]),
    ]
    for copy in local:
        copy.start()

    barrier = pltpu.get_barrier_semaphore()

    def greet(device):
        pl.semaphore_signal(barrier, inc=1, device_id=device, device_id_type=MESH)

    for d in range(1, NX):
        greet(at_x(d))
    for d in range(1, NY):
        greet(at_y(d))
    for d in range(1, NZ):
        greet(at_z(d))
    greet(partner)

    @pl.when(row != col)
    def _():
        greet((col, row))
        pl.semaphore_wait(barrier, 15)

    @pl.when(row == col)
    def _():
        pl.semaphore_wait(barrier, 14)

    local[0].wait()
    local[1].wait()

    rings = {"x": at_x, "y": at_y}

    def piece(ring, item, shift):
        if ring == "x":
            owner_x, owner_y = lax.rem(x + shift + NX, NX), y if item == 0 else lax.rem(y + item - 1, NY)
            offset = 0 if item == 0 else PIECE
        else:
            owner_y, owner_x = lax.rem(y + shift + NY, NY), x if item == 0 else lax.rem(x + item - 1, NX)
            offset = PIECE if item == 0 else 0
        return pl.ds(pl.multiple_of((owner_y * NX + owner_x) * CHUNK + offset, 8), PIECE)

    full, halves = {}, {}

    def send(ring, item):
        rows = f_all.at[piece(ring, item, 0)]
        full[ring, item] = [push(rows, rows, rings[ring](1)), push(rows, rows, rings[ring](-1))]

    def forward(ring, item):
        from_left, from_right = full[ring, item]
        from_left.wait_recv()
        rows = f_all.at[piece(ring, item, -1), pl.ds(0, 512)]
        right = push(rows, rows, rings[ring](1))
        from_right.wait_recv()
        rows = f_all.at[piece(ring, item, 1), pl.ds(512, 512)]
        halves[ring, item] = [right, push(rows, rows, rings[ring](-1))]

    def settle(ring, item):
        for copy in halves[ring, item]:
            copy.wait_recv()

    send("x", 0), send("y", 0), send("x", 1), send("y", 1)
    grad_copy = push(gbuf.at[pl.ds(aligned(k, 64), 64)], gbuf.at[pl.ds(aligned(k, 64), 64)], partner)

    local[3].wait()
    inverse_diagonals(low, inv)
    forward("x", 0), forward("y", 0)
    send("x", 2), send("y", 2), send("x", 4), send("y", 4)
    local[2].wait()

    @pl.loop(0, 8)
    def _(step):
        rows = pl.ds(aligned(step, 128), 128)
        s_high[rows], s_low[rows] = split(strail[rows])

    forward("x", 1), forward("y", 1)
    settle("x", 0), settle("y", 0)
    send("x", 3), send("y", 3)
    inverse_blocks(low, inv)
    forward("x", 2), forward("y", 2), forward("x", 4), forward("y", 4)
    settle("x", 1)

    def multiply(j):
        rows = pl.ds(aligned(lax.rem(y + j, NY), GROUP), GROUP)
        f_high, f_low = split(f_all[rows])

        @pl.loop(0, 4)
        def _(step):
            part = pl.ds(aligned(step, BLOCK), BLOCK)
            dims = ((1,), (1,))
            zt[j, :, part] = (
                contract(f_low, s_high[part], dims) + contract(f_high, s_low[part], dims) + contract(f_high, s_high[part], dims)
            )

    crossing = {}

    def cross(j):
        crossing[j] = push(zt.at[j, pl.ds(aligned(other, SUB), SUB)], cx.at[j], partner)

    lefts, rights = {}, {}

    def begin(j):
        crossing[j].wait_recv()
        own = pl.ds(aligned(k, SUB), SUB)
        for d in range(NZ):
            lanes = pl.ds(128 * d, 128)
            zc[j, d] = zt[j, own, lanes] + cx[j, :, lanes]
        far = lax.rem(z + 4, NZ)
        lefts[j] = push(zc.at[j, far, pl.ds(0, 48)], r_left.at[j, 0, pl.ds(0, 48)], at_z(-1))
        rights[j] = push(zc.at[j, far, pl.ds(48, 48)], r_right.at[j, 0, pl.ds(48, 48)], at_z(1))

    def travel(j, step):
        to_left, to_right = lax.rem(z + 3 + step, NZ), lax.rem(z + 5 - step, NZ)
        lefts[j].wait_recv()
        if step == 2:
            zc[j, to_left, 0:48] += r_left[j, 0, 0:48]
        else:
            zc[j, to_left] += r_left[j, step - 2]
        lefts[j] = push(zc.at[j, to_left], r_left.at[j, step - 1], at_z(-1))
        rights[j].wait_recv()
        if step == 2:
            zc[j, to_right, 48:96] += r_right[j, 0, 48:96]
        else:
            zc[j, to_right] += r_right[j, step - 2]
        rights[j] = push(zc.at[j, to_right], r_right.at[j, step - 1], at_z(1))

    shares = []

    def arrive(j):
        lefts[j].wait_recv()
        rights[j].wait_recv()
        rows = pl.ds(pl.multiple_of(lax.rem(y + j, NY) * GROUP + k * SUB, 8), SUB)
        p_hat[rows] = p_hat[rows] - 2.0 * (zc[j, z] + r_left[j, 3] + r_right[j, 3])
        shares.append(push(p_hat.at[rows], p_hat.at[rows], partner))

    multiply(0)
    cross(0)
    forward("x", 3), forward("y", 3)
    begin(0)
    settle("x", 2), settle("x", 4)
    multiply(1)
    cross(1)
    travel(0, 2)
    multiply(3)
    cross(3)
    begin(1)
    travel(0, 3)
    for ring, item in (("y", 1), ("y", 2), ("y", 3), ("y", 4), ("x", 3)):
        settle(ring, item)
    begin(3)
    travel(0, 4)
    travel(1, 2)
    multiply(2)
    cross(2)
    half, tile = lax.rem(row, 2), lax.div(row, 2)

    def transposed(block):
        return f_all.at[pl.ds(pl.multiple_of(block * BLOCK + half * HALF, HALF), HALF), pl.ds(aligned(tile, HALF), HALF)]

    moves = [
        pltpu.make_async_remote_copy(
            src_ref=transposed(block), dst_ref=f_own.at[block], send_sem=send_sem.at[SEMAPHORES - 1 - block],
            recv_sem=recv_sem.at[SEMAPHORES - 1 - block], device_id=(col, row), device_id_type=MESH,
        )
        for block in range(3)
    ]
    stays = [pltpu.make_async_copy(transposed(block), f_own.at[block], local_sem.at[5 + block]) for block in range(3)]

    @pl.when(row != col)
    def _():
        for copy in moves:
            copy.start()

    @pl.when(row == col)
    def _():
        for copy in stays:
            copy.start()

    travel(3, 2)
    begin(2)
    travel(1, 3)
    travel(3, 3)
    travel(2, 2)
    grad_copy.wait_recv()
    own_rows = pl.ds(aligned(k, SUB), SUB)
    gt = gbuf[...].T
    cmat[:, 0:128] = gt
    for j in range(4):
        rows = pl.ds(pl.multiple_of(j * GROUP + k * SUB, 8), SUB)
        p_hat[rows] = cmat[rows, 0:128]
    arrive(0)
    travel(1, 4)
    travel(3, 4)
    travel(2, 3)
    arrive(1)
    arrive(3)
    travel(2, 4)
    local[4].wait()
    start_gradient(low, topv, cmat)
    arrive(2)
    for copy in shares:
        copy.wait_recv()

    @pl.when(row != col)
    def _():
        for copy in moves:
            copy.wait()

    @pl.when(row == col)
    def _():
        for copy in stays:
            copy.wait()

    for block in range(3):
        start = OFFSETS[block]
        rows = WIDTH - BLOCK * block
        wst[start : start + rows] = dot3(p_hat[BLOCK * block :], f_own[block], ((1,), (1,)))

    def scatter(src, unit, extent, reach, me, buffer):
        copies = []
        for d in range(1, extent):
            to = lax.rem(me + d, extent)
            copies.append(push(src(to), buffer.at[d - 1], reach(d)))
        return copies

    def total(own, copies, buffer):
        for d, copy in enumerate(copies):
            copy.wait_recv()
            own = own + buffer[d]
        return own

    def gather(ref, extent, reach):
        return [push(ref, ref, reach(d)) for d in range(1, extent)]

    def arrived(copies):
        for copy in copies:
            copy.wait_recv()

    def rows_of(base, start, size):
        return pl.ds(pl.multiple_of(base + start, 8), size)

    sc = scatter(lambda to: wst.at[rows_of(1024, to * 64, 64)], 64, NZ, at_z, z, r_c1)
    sa = scatter(lambda to: wst.at[rows_of(0, to * 128, 128)], 128, NX, at_x, x, r_a1)
    sb = scatter(lambda to: wst.at[rows_of(512, to * 128, 128)], 128, NY, at_y, y, r_b1)
    p_rows[...] = p_hat[...].T
    a1[...] = total(wst[rows_of(0, x * 128, 128)], sa, r_a1)
    sa = scatter(lambda to: a1.at[rows_of(0, to * 32, 32)], 32, NY, at_y, y, r_a2)
    b1[...] = total(wst[rows_of(512, y * 128, 128)], sb, r_b1)
    sb = scatter(lambda to: b1.at[rows_of(0, to * 32, 32)], 32, NX, at_x, x, r_b2)
    a2[z] = total(a1[rows_of(0, y * 32, 32)], sa, r_a2)
    sa = gather(a2.at[z], NZ, at_z)
    b2[z] = total(b1[rows_of(0, x * 32, 32)], sb, r_b2)
    sb = gather(b2.at[z], NZ, at_z)
    c1[...] = total(wst[rows_of(1024, z * 64, 64)], sc, r_c1)
    sc = scatter(lambda to: c1.at[rows_of(0, to * 16, 16)], 16, NX, at_x, x, r_c2)
    c2[y] = total(c1[rows_of(0, x * 16, 16)], sc, r_c2)
    sc = gather(c2.at[y], NY, at_y)
    inverse_transposed(inv, inv_t)
    arrived(sc)
    rows = rows_of(1024, z * 64 + x * 16, 16)
    wfull[k, rows] = c2[0] + c2[1] + c2[2] + c2[3]
    sc = gather(wfull.at[k, rows], NX, at_x)

    def over_z(ref):
        value = ref[0]
        for d in range(1, NZ):
            value = value + ref[d]
        return value

    arrived(sa)
    rows = rows_of(0, x * 128 + y * 32, 32)
    wfull[k, rows] = over_z(a2)
    sa = gather(wfull.at[k, rows], NY, at_y)
    arrived(sb)
    rows = rows_of(512, y * 128 + x * 32, 32)
    wfull[k, rows] = over_z(b2)
    sb = gather(wfull.at[k, rows], NX, at_x)
    arrived(sc)
    sc = gather(wfull.at[k, rows_of(1024, z * 64, 64)], NZ, at_z)
    arrived(sa)
    sa = gather(wfull.at[k, rows_of(0, x * 128, 128)], NX, at_x)
    arrived(sb)
    sb = gather(wfull.at[k, rows_of(512, y * 128, 128)], NY, at_y)
    out_rows[...] = dot6(p_rows[pl.ds(aligned(k, 64), 64)], inv[...])
    finals = []
    for start, copies in ((0, sa), (512, sb), (1024, sc)):
        arrived(copies)
        third = wfull.at[k, pl.ds(start, 512)]
        finals.append(push(third, third, partner))
    arrived(finals)
    finish_gradient(inv, inv_t, cmat, wfull, mmat, xmat, out_top)
    for copy in pending:
        copy.wait_send()


def inverse_diagonals(low, inv):
    rows, lanes = iota((HALF, HALF), 0), iota((HALF, HALF), 1)
    group = rows - lax.rem(rows, 8)

    @pl.loop(0, 6)
    def _(block):
        span = pl.ds(aligned(block, HALF), HALF)
        own = low[span, span]
        within = iota((16, 8, HALF), 1)
        value = jnp.where(rows == lanes, 1.0, 0.0).reshape(16, 8, HALF)
        for step in range(8):
            column = jnp.sum(jnp.where(lanes == group + step, own, 0.0), axis=1, keepdims=True)
            column = jnp.broadcast_to(column, (HALF, HALF)).reshape(16, 8, HALF)
            solved = value[:, step : step + 1] / column[:, step : step + 1]
            solved = jnp.broadcast_to(solved, (16, 8, HALF))
            value = jnp.where(within == step, solved, jnp.where(within > step, value - column * solved, value))
        value = value.reshape(HALF, HALF)
        for size in (8, 16, 32, 64):
            upper, left = lax.div(rows, size), lax.div(lanes, size)
            mask = jnp.logical_and(left + 1 == upper, lax.rem(upper, 2) == 1)
            value = value - dot6(value, dot6(jnp.where(mask, own, 0.0), value))
        inv[span, span] = value


def inverse_blocks(low, inv):
    zero = jnp.zeros((HALF, HALF), F32)
    for block in range(3):
        first, second = slice(block * BLOCK, block * BLOCK + HALF), slice(block * BLOCK + HALF, block * BLOCK + BLOCK)
        inv[second, first] = -dot6(inv[second, second], dot6(low[second, first], inv[first, first]))
        inv[first, second] = zero
    one, two, three = slice(0, BLOCK), slice(BLOCK, 2 * BLOCK), slice(2 * BLOCK, 3 * BLOCK)
    inv[two, one] = -dot6(inv[two, two], dot6(low[two, one], inv[one, one]))
    inv[three, two] = -dot6(inv[three, three], dot6(low[three, two], inv[two, two]))
    inv[three, one] = -dot6(
        inv[three, three], dot6(low[three, one], inv[one, one]) + dot6(low[three, two], inv[two, one])
    )
    inv[one, 256:768] = jnp.zeros((BLOCK, 512), F32)
    inv[two, 512:768] = jnp.zeros((BLOCK, BLOCK), F32)


def inverse_transposed(inv, inv_t):
    for i in range(3):
        for j in range(i, 3):
            rows, lanes = slice(BLOCK * i, BLOCK * i + BLOCK), slice(BLOCK * j, BLOCK * j + BLOCK)
            inv_t[rows, lanes] = inv[lanes, rows].T


def start_gradient(low, topv, cmat):
    rows, lanes = iota((BLOCK, BLOCK), 0), iota((BLOCK, BLOCK), 1)
    for i in range(3):
        block = slice(BLOCK * i, BLOCK * i + BLOCK)
        flipped = low[BLOCK * i :, block].T
        for j in range(3):
            other = slice(BLOCK * j, BLOCK * j + BLOCK)
            if j > i:
                cmat[block, other] = jnp.zeros((BLOCK, BLOCK), F32)
                continue
            value = dot3(flipped, topv[BLOCK * i :, other])
            if i == j:
                value = jnp.where(rows > lanes, value, jnp.where(rows == lanes, 0.5 * value, 0.0))
            cmat[block, other] = value


def finish_gradient(inv, inv_t, cmat, wfull, mmat, xmat, out_top):
    rows, lanes = iota((BLOCK, HALF), 0), iota((BLOCK, HALF), 1)
    for block in range(3):
        for side in range(2):
            start = OFFSETS[block]
            column = slice(BLOCK * block + HALF * side, BLOCK * block + HALF * side + HALF)
            value = wfull[side, start : start + BLOCK]
            place = lanes + HALF * side
            value = jnp.where(rows > place, value, jnp.where(rows == place, 0.5 * value, 0.0))
            cmat[BLOCK * block : BLOCK * block + BLOCK, column] -= value
            if block < 2:
                end = start + WIDTH - BLOCK * block
                cmat[BLOCK * block + BLOCK :, column] -= wfull[side, start + BLOCK : end]
    for i in range(3):
        block = slice(BLOCK * i, BLOCK * i + BLOCK)
        mmat[block] = dot3(inv_t[block, BLOCK * i :], cmat[BLOCK * i :])
    for j in range(3):
        block = slice(BLOCK * j, BLOCK * j + BLOCK)
        xmat[:, block] = dot3(mmat[:, BLOCK * j :], inv[BLOCK * j :, block])
    rows, lanes = iota((BLOCK, BLOCK), 0), iota((BLOCK, BLOCK), 1)
    for i in range(3):
        for j in range(3):
            block, other = slice(BLOCK * i, BLOCK * i + BLOCK), slice(BLOCK * j, BLOCK * j + BLOCK)
            if j > i:
                out_top[block, other] = jnp.zeros((BLOCK, BLOCK), F32)
                continue
            value = xmat[block, other] + xmat[other, block].T
            if i == j:
                value = jnp.where(rows > lanes, value, jnp.where(rows == lanes, 0.5 * value, 0.0))
            out_top[block, other] = value


def per_device(trail_grad, factor_rows, factor_top, rows_grad, top_grad):
    anywhere = pl.BlockSpec(memory_space=pl.ANY)
    inside = pl.BlockSpec(memory_space=pltpu.VMEM)
    square = pltpu.VMEM((WIDTH, WIDTH), F32)

    def vmem(*shape):
        return pltpu.VMEM(shape, F32)

    return pl.pallas_call(
        kernel,
        out_shape=(jax.ShapeDtypeStruct((64, WIDTH), F32), jax.ShapeDtypeStruct((WIDTH, WIDTH), F32)),
        in_specs=[anywhere] * 5,
        out_specs=(inside, inside),
        scratch_shapes=[
            vmem(1024, 1024), pltpu.VMEM((1024, 1024), BF16), pltpu.VMEM((1024, 1024), BF16),
            vmem(WIDTH, 1024), vmem(4, GROUP, 1024), vmem(4, SUB, 1024), vmem(4, 8, SUB, 128), vmem(4, 4, SUB, 128),
            vmem(4, 4, SUB, 128), square, square, square, square, square, square, square, vmem(128, WIDTH), vmem(WIDTH, 128),
            vmem(128, WIDTH), vmem(3, 128, 128), vmem(1536, 128), vmem(3, 128, 128), vmem(3, 32, 128), vmem(128, 128),
            vmem(8, 32, 128), vmem(3, 128, 128), vmem(3, 32, 128), vmem(128, 128), vmem(8, 32, 128), vmem(7, 64, 128),
            vmem(3, 16, 128), vmem(64, 128), vmem(4, 16, 128), vmem(2, 1536, 128), pltpu.SemaphoreType.DMA((8,)),
            pltpu.SemaphoreType.DMA((SEMAPHORES,)), pltpu.SemaphoreType.DMA((SEMAPHORES,)),
        ],
        compiler_params=pltpu.CompilerParams(collective_id=0, has_side_effects=True, vmem_limit_bytes=62 << 20),
    )(trail_grad, factor_rows.T, factor_top, rows_grad, top_grad)


def solution(mesh):
    placed = (P("row", "col"), P("col", "row"), P(), P(("row", "col"), None), P())
    return jax.shard_map(
        per_device,
        mesh=mesh,
        in_specs=placed,
        out_specs=(P(("row", "col"), None), P()),
        check_vma=False,
    )
```

time: 648 us -> 131 us (0.20); the launches traced: 638 us -> 130 us
  waiting for transfers between devices: 448 us -> 0 us
  Pallas kernels: 0 us -> 125 us
  matrix products: 72.5 us -> 0 us
  other arithmetic: 67.5 us -> 0 us
  local copies, waits for them, and re-layouts: 34.5 us -> 4.84 us
  between operations: 14.9 us -> 0.64 us
    psum x1 -> x0, waiting for transfers between devices: 262 us -> none  [per_device(): lax.psum(column_products(rows_adj, cross_factor[:, col_start:col_end]), (...]
    reduce_scatter x4 -> x0, waiting for transfers between devices: 127 us -> none  [the longest x3 67.4 us: per_device(): lax.psum_scatter(partial_rows, 'col', scatter_dimension=0, tiled=True)]
    pallas_call x0 -> x1, Pallas kernels: none -> 125 us  [per_device(): pl.pallas_call(kernel, out_shape=(jax.ShapeDtypeStruct((64, WIDTH), F32),...]
    dot_general x33 -> x0, matrix products: 67.3 us -> none  [the longest x26 55.2 us: product(): jnp.dot(left, right, precision=exact_dots, preferred_element_type=jnp.flo...]
    another operation x10 -> x0, other arithmetic: 64.6 us -> none  [the longest x5 60.3 us: per_device(): jax.scipy.linalg.solve_triangular(diag_block, identity, lower=True)]
    all_gather x1 -> x0, waiting for transfers between devices: 58.4 us -> none  [per_device(): panels = lax.all_gather(factor_rows, 'row', axis=1, tiled=True)]
    another operation x24 -> x0, local copies, waits for them, and re-layouts: 12.6 us -> none  [the longest x23 11.2 us: per_device(): jax.scipy.linalg.solve_triangular(diag_block, identity, lower=True)]
    dot_general x5 -> x0, local copies, waits for them, and re-layouts: 6.73 us -> none  [the longest x4 4.14 us: product(): jnp.dot(left, right, precision=exact_dots, preferred_element_type=jnp.flo...]
  transfers between devices with their start and end apart: 6 -> 0, of which waited for: 5 -> 0; matrix products, arithmetic and copies ran while one was open for 17% -> 0% of each run, Pallas kernels for 0% -> 0%
where the time goes in v1:
time: 131 us; the launch traced here: 130 us
  Pallas kernels  125 us (95%)
  local copies, waits for them, and re-layouts  4.84 us (4%)
    pallas_call x1, Pallas kernels, per_device(): pl.pallas_call(kernel, out_shape=(jax.ShapeDtypeStruct((64, WIDTH), F32),...  125 us
    unnamed x2, local copies, waits for them, and re-layouts  4.84 us

profile of v1, /device:TPU:1, one launch (start us, length us, event | category | flops | bytes accessed | tf_op | source)
XLA Modules:
  0.0 130.5 jit_solution(15431963461499121900)
XLA Ops:
  0.6 125.0 %shard_map.68 = (f32[64,768]{1,0:T(8,128)}, f32[768,768]{1,0:T(8,128)}) custom-call(f32[1024,1024]{1,0:T(8,128)} %trail.1, f32[48,1024]{1,0:T(8,128)} %bitcast.1, f32[768,768]{1,0:T(8,128)} %lower.1, f32[64,768]{1,0:T(8,128)} %grad.1, f32[768,768]{1,0:T(8,128)} %top.1), custom_call_target="tpu_custom_call" | custom-call | tf_op jit(solution)/shard_map/pallas_call | solution.py:483
  125.7 1.6 %copy.9 = f32[64,768]{1,0:T(8,128)} copy(f32[64,768]{1,0:T(8,128)} %get-tuple-element.4) | data formatting | bytes 393216
  127.3 3.2 %copy.10 = f32[768,768]{1,0:T(8,128)} copy(f32[768,768]{1,0:T(8,128)} %get-tuple-element.5) | data formatting | bytes 4718592

commit v2 on v1

--- a/solution.py
+++ b/solution.py
@@ -48,7 +48,7 @@
 
 
 def kernel(trail, factor, lower, grad, top, out_rows, out_top, strail, s_high, s_low, f_all, zt, cx, zc, r_left, r_right, low, topv,
-           inv, inv_t, cmat, mmat, xmat, gbuf, p_hat, p_rows, f_own, wst, r_a1, r_a2, a1, a2, r_b1, r_b2, b1, b2, r_c1, r_c2, c1, c2,
+           inv, inv_t, cmat, mmat, xmat, gbuf, p_hat, p_rows, planes, f_here, wst, r_a1, r_a2, a1, a2, r_b1, r_b2, b1, b2, r_c1, r_c2, c1, c2,
            wfull, local_sem, send_sem, recv_sem):
     row, col = lax.axis_index("row"), lax.axis_index("col")
     y, x = lax.div(row, NX), lax.rem(row, NX)
@@ -93,22 +93,12 @@
     def greet(device):
         pl.semaphore_signal(barrier, inc=1, device_id=device, device_id_type=MESH)
 
-    for d in range(1, NX):
-        greet(at_x(d))
-    for d in range(1, NY):
-        greet(at_y(d))
+    for d in range(1, NX * NY):
+        greet((lax.rem(row + d, NX * NY), col))
     for d in range(1, NZ):
         greet(at_z(d))
     greet(partner)
-
-    @pl.when(row != col)
-    def _():
-        greet((col, row))
-        pl.semaphore_wait(barrier, 15)
-
-    @pl.when(row == col)
-    def _():
-        pl.semaphore_wait(barrier, 14)
+    pl.semaphore_wait(barrier, NX * NY + NZ - 1)
 
     local[0].wait()
     local[1].wait()
@@ -144,12 +134,77 @@
             copy.wait_recv()
 
     send("x", 0), send("y", 0), send("x", 1), send("y", 1)
-    grad_copy = push(gbuf.at[pl.ds(aligned(k, 64), 64)], gbuf.at[pl.ds(aligned(k, 64), 64)], partner)
-
-    local[3].wait()
-    inverse_diagonals(low, inv)
-    forward("x", 0), forward("y", 0)
-    send("x", 2), send("y", 2), send("x", 4), send("y", 4)
+    own_half = pl.ds(aligned(k, 64), 64)
+    grad_copy = push(gbuf.at[own_half], gbuf.at[own_half], partner)
+    chunk = pl.ds(aligned(row, CHUNK), CHUNK)
+    spread = []
+    for d in range(1, NZ):
+        lanes = pl.ds(aligned(lax.rem(z + d, NZ), 128), 128)
+        spread.append(push(f_all.at[chunk, lanes], planes.at[z], at_z(d)))
+    keep = pltpu.make_async_copy(f_all.at[chunk, pl.ds(aligned(z, 128), 128)], planes.at[z], local_sem.at[5])
+    keep.start()
+    owner = lax.rem(row, 2) == k
+    landing = f_here.at[chunk]
+    pair = lax.div(row, 2)
+    exchange, first_move, first_stay = [], [], []
+
+    def rearrange():
+        keep.wait()
+        for copy in spread:
+            copy.wait_recv()
+        for d in range(NZ):
+            block = lax.rem(pair + d, NZ)
+            copy = pltpu.make_async_remote_copy(
+                src_ref=planes.at[block], dst_ref=landing, send_sem=send_sem.at[SEMAPHORES - 2 - d],
+                recv_sem=recv_sem.at[SEMAPHORES - 1], device_id=(block * 2 + k, col), device_id_type=MESH,
+            )
+            if d == 0:
+                first_move.append(copy)
+                first_stay.append(pltpu.make_async_copy(planes.at[block], landing, local_sem.at[6]))
+            else:
+                copy.start()
+                exchange.append(copy)
+
+        @pl.when(jnp.logical_not(owner))
+        def _():
+            first_move[0].start()
+
+        @pl.when(owner)
+        def _():
+            first_stay[0].start()
+
+    share = pltpu.make_async_remote_copy(
+        src_ref=f_here, dst_ref=f_here, send_sem=send_sem.at[SEMAPHORES - 10], recv_sem=recv_sem.at[SEMAPHORES - 10],
+        device_id=partner, device_id_type=MESH,
+    )
+
+    def pass_on():
+        for copy in exchange:
+            copy.wait_send()
+
+        @pl.when(owner)
+        def _():
+            most = f_here.at[0 : WIDTH - CHUNK]
+            pltpu.make_async_remote_copy(
+                src_ref=most, dst_ref=most, send_sem=send_sem.at[SEMAPHORES - 1], recv_sem=recv_sem.at[SEMAPHORES - 1],
+                device_id=partner, device_id_type=MESH,
+            ).wait_recv()
+            first_stay[0].wait()
+            share.start()
+
+        @pl.when(jnp.logical_not(owner))
+        def _():
+            first_move[0].wait_send()
+
+    def passed():
+        @pl.when(owner)
+        def _():
+            share.wait_send()
+
+        @pl.when(jnp.logical_not(owner))
+        def _():
+            share.wait_recv()
+
     local[2].wait()
 
     @pl.loop(0, 8)
@@ -157,11 +212,20 @@
         rows = pl.ds(aligned(step, 128), 128)
         s_high[rows], s_low[rows] = split(strail[rows])
 
+    forward("x", 0), forward("y", 0)
+    send("x", 2), send("y", 2), send("x", 4), send("y", 4)
+    local[3].wait()
+    inverse_pair(low, inv, 0)
     forward("x", 1), forward("y", 1)
     settle("x", 0), settle("y", 0)
     send("x", 3), send("y", 3)
-    inverse_blocks(low, inv)
+    inverse_pair(low, inv, 1)
     forward("x", 2), forward("y", 2), forward("x", 4), forward("y", 4)
+    grad_copy.wait_recv()
+    cmat[:, 0:128] = gbuf[...].T
+    for j in range(4):
+        rows = pl.ds(pl.multiple_of(j * GROUP + k * SUB, 8), SUB)
+        p_hat[rows] = cmat[rows, 0:128]
     settle("x", 1)
 
     def multiply(j):
@@ -220,6 +284,7 @@
     multiply(0)
     cross(0)
     forward("x", 3), forward("y", 3)
+    rearrange()
     begin(0)
     settle("x", 2), settle("x", 4)
     multiply(1)
@@ -231,74 +296,36 @@
     travel(0, 3)
     for ring, item in (("y", 1), ("y", 2), ("y", 3), ("y", 4), ("x", 3)):
         settle(ring, item)
+    multiply(2)
+    cross(2)
     begin(3)
     travel(0, 4)
     travel(1, 2)
-    multiply(2)
-    cross(2)
-    half, tile = lax.rem(row, 2), lax.div(row, 2)
-
-    def transposed(block):
-        return f_all.at[pl.ds(pl.multiple_of(block * BLOCK + half * HALF, HALF), HALF), pl.ds(aligned(tile, HALF), HALF)]
-
-    moves = [
-        pltpu.make_async_remote_copy(
-            src_ref=transposed(block), dst_ref=f_own.at[block], send_sem=send_sem.at[SEMAPHORES - 1 - block],
-            recv_sem=recv_sem.at[SEMAPHORES - 1 - block], device_id=(col, row), device_id_type=MESH,
-        )
-        for block in range(3)
-    ]
-    stays = [pltpu.make_async_copy(transposed(block), f_own.at[block], local_sem.at[5 + block]) for block in range(3)]
-
-    @pl.when(row != col)
-    def _():
-        for copy in moves:
-            copy.start()
-
-    @pl.when(row == col)
-    def _():
-        for copy in stays:
-            copy.start()
-
+    pass_on()
+    begin(2)
     travel(3, 2)
-    begin(2)
     travel(1, 3)
+    travel(2, 2)
+    arrive(0)
     travel(3, 3)
-    travel(2, 2)
-    grad_copy.wait_recv()
-    own_rows = pl.ds(aligned(k, SUB), SUB)
-    gt = gbuf[...].T
-    cmat[:, 0:128] = gt
-    for j in range(4):
-        rows = pl.ds(pl.multiple_of(j * GROUP + k * SUB, 8), SUB)
-        p_hat[rows] = cmat[rows, 0:128]
-    arrive(0)
     travel(1, 4)
+    travel(2, 3)
+    inverse_pair(low, inv, 2)
+    arrive(1)
     travel(3, 4)
-    travel(2, 3)
-    arrive(1)
+    travel(2, 4)
     arrive(3)
-    travel(2, 4)
     local[4].wait()
     start_gradient(low, topv, cmat)
     arrive(2)
     for copy in shares:
         copy.wait_recv()
-
-    @pl.when(row != col)
-    def _():
-        for copy in moves:
-            copy.wait()
-
-    @pl.when(row == col)
-    def _():
-        for copy in stays:
-            copy.wait()
+    passed()
 
     for block in range(3):
         start = OFFSETS[block]
         rows = WIDTH - BLOCK * block
-        wst[start : start + rows] = dot3(p_hat[BLOCK * block :], f_own[block], ((1,), (1,)))
+        wst[start : start + rows] = dot3(p_hat[BLOCK * block :], f_here[pl.ds(pl.multiple_of(block * BLOCK + k * HALF, HALF), HALF)], ((1,), (1,)))
 
     def scatter(src, unit, extent, reach, me, buffer):
         copies = []
@@ -339,6 +366,7 @@
     sc = scatter(lambda to: c1.at[rows_of(0, to * 16, 16)], 16, NX, at_x, x, r_c2)
     c2[y] = total(c1[rows_of(0, x * 16, 16)], sc, r_c2)
     sc = gather(c2.at[y], NY, at_y)
+    inverse_blocks(low, inv)
     inverse_transposed(inv, inv_t)
     arrived(sc)
     rows = rows_of(1024, z * 64 + x * 16, 16)
@@ -377,36 +405,44 @@
         copy.wait_send()
 
 
-def inverse_diagonals(low, inv):
+def odd(value, size):
+    return value.reshape(HALF // (2 * size), 2, size, HALF)[:, 1].reshape(HALF // 2, HALF)
+
+
+def inverse_pair(low, inv, which):
     rows, lanes = iota((HALF, HALF), 0), iota((HALF, HALF), 1)
     group = rows - lax.rem(rows, 8)
-
-    @pl.loop(0, 6)
-    def _(block):
-        span = pl.ds(aligned(block, HALF), HALF)
-        own = low[span, span]
-        within = iota((16, 8, HALF), 1)
-        value = jnp.where(rows == lanes, 1.0, 0.0).reshape(16, 8, HALF)
-        for step in range(8):
-            column = jnp.sum(jnp.where(lanes == group + step, own, 0.0), axis=1, keepdims=True)
+    within = iota((16, 8, HALF), 1)
+    spans = [slice(which * BLOCK + HALF * i, which * BLOCK + HALF * i + HALF) for i in range(2)]
+    owns = [low[span, span] for span in spans]
+    values = [jnp.where(rows == lanes, 1.0, 0.0).reshape(16, 8, HALF)] * 2
+    for step in range(8):
+        for i in range(2):
+            value = values[i]
+            column = jnp.sum(jnp.where(lanes == group + step, owns[i], 0.0), axis=1, keepdims=True)
             column = jnp.broadcast_to(column, (HALF, HALF)).reshape(16, 8, HALF)
             solved = value[:, step : step + 1] / column[:, step : step + 1]
             solved = jnp.broadcast_to(solved, (16, 8, HALF))
-            value = jnp.where(within == step, solved, jnp.where(within > step, value - column * solved, value))
-        value = value.reshape(HALF, HALF)
-        for size in (8, 16, 32, 64):
-            upper, left = lax.div(rows, size), lax.div(lanes, size)
-            mask = jnp.logical_and(left + 1 == upper, lax.rem(upper, 2) == 1)
-            value = value - dot6(value, dot6(jnp.where(mask, own, 0.0), value))
-        inv[span, span] = value
+            values[i] = jnp.where(within == step, solved, jnp.where(within > step, value - column * solved, value))
+    values = [value.reshape(HALF, HALF) for value in values]
+    for size in (8, 16, 32, 64):
+        upper, left = lax.div(rows, size), lax.div(lanes, size)
+        mask = jnp.logical_and(left + 1 == upper, lax.rem(upper, 2) == 1)
+        inner = [dot6(odd(jnp.where(mask, owns[i], 0.0), size), values[i]) for i in range(2)]
+        shape = (HALF // (2 * size), 1, size, HALF)
+        none = jnp.zeros(shape, F32)
+        inner = [jnp.concatenate([none, value.reshape(shape)], axis=1).reshape(HALF, HALF) for value in inner]
+        inner = [dot6(odd(values[i], size), inner[i]) for i in range(2)]
+        inner = [jnp.concatenate([none, value.reshape(shape)], axis=1).reshape(HALF, HALF) for value in inner]
+        values = [values[i] - inner[i] for i in range(2)]
+    first, second = spans
+    inv[first, first] = values[0]
+    inv[second, second] = values[1]
+    inv[second, first] = -dot6(values[1], dot6(low[second, first], values[0]))
+    inv[first, second] = jnp.zeros((HALF, HALF), F32)
 
 
 def inverse_blocks(low, inv):
-    zero = jnp.zeros((HALF, HALF), F32)
-    for block in range(3):
-        first, second = slice(block * BLOCK, block * BLOCK + HALF), slice(block * BLOCK + HALF, block * BLOCK + BLOCK)
-        inv[second, first] = -dot6(inv[second, second], dot6(low[second, first], inv[first, first]))
-        inv[first, second] = zero
     one, two, three = slice(0, BLOCK), slice(BLOCK, 2 * BLOCK), slice(2 * BLOCK, 3 * BLOCK)
     inv[two, one] = -dot6(inv[two, two], dot6(low[two, one], inv[one, one]))
     inv[three, two] = -dot6(inv[three, three], dot6(low[three, two], inv[two, two]))
@@ -489,7 +525,7 @@
             vmem(1024, 1024), pltpu.VMEM((1024, 1024), BF16), pltpu.VMEM((1024, 1024), BF16),
             vmem(WIDTH, 1024), vmem(4, GROUP, 1024), vmem(4, SUB, 1024), vmem(4, 8, SUB, 128), vmem(4, 4, SUB, 128),
             vmem(4, 4, SUB, 128), square, square, square, square, square, square, square, vmem(128, WIDTH), vmem(WIDTH, 128),
-            vmem(128, WIDTH), vmem(3, 128, 128), vmem(1536, 128), vmem(3, 128, 128), vmem(3, 32, 128), vmem(128, 128),
+            vmem(128, WIDTH), vmem(NZ, CHUNK, 128), vmem(WIDTH, 128), vmem(1536, 128), vmem(3, 128, 128), vmem(3, 32, 128), vmem(128, 128),
             vmem(8, 32, 128), vmem(3, 128, 128), vmem(3, 32, 128), vmem(128, 128), vmem(8, 32, 128), vmem(7, 64, 128),
             vmem(3, 16, 128), vmem(64, 128), vmem(4, 16, 128), vmem(2, 1536, 128), pltpu.SemaphoreType.DMA((8,)),
             pltpu.SemaphoreType.DMA((SEMAPHORES,)), pltpu.SemaphoreType.DMA((SEMAPHORES,)),

time: 131 us -> 100 us (0.76)
  Pallas kernels: 125 us -> 94.7 us
    pallas_call x1, Pallas kernels: 125 us -> 94.7 us  [per_device(): pl.pallas_call(kernel, out_shape=(jax.ShapeDtypeStruct((64, WIDTH), F32),...]
where the time goes in v2:
time: 100 us
  Pallas kernels  94.7 us (95%)
  local copies, waits for them, and re-layouts  4.84 us (5%)
    pallas_call x1, Pallas kernels, per_device(): pl.pallas_call(kernel, out_shape=(jax.ShapeDtypeStruct((64, WIDTH), F32),...  94.7 us
    unnamed x2, local copies, waits for them, and re-layouts  4.84 us

profile of v2, /device:TPU:1, one launch (start us, length us, event | category | flops | bytes accessed | tf_op | source)
XLA Modules:
  0.0 100.2 jit_solution(12016607196734994119)
XLA Ops:
  0.6 94.7 %shard_map.68 = (f32[64,768]{1,0:T(8,128)}, f32[768,768]{1,0:T(8,128)}) custom-call(f32[1024,1024]{1,0:T(8,128)} %trail.1, f32[48,1024]{1,0:T(8,128)} %bitcast.1, f32[768,768]{1,0:T(8,128)} %lower.1, f32[64,768]{1,0:T(8,128)} %grad.1, f32[768,768]{1,0:T(8,128)} %top.1), custom_call_target="tpu_custom_call" | custom-call | tf_op jit(solution)/shard_map/pallas_call | solution.py:519
  95.3 1.6 %copy.9 = f32[64,768]{1,0:T(8,128)} copy(f32[64,768]{1,0:T(8,128)} %get-tuple-element.4) | data formatting | bytes 393216
  97.0 3.2 %copy.10 = f32[768,768]{1,0:T(8,128)} copy(f32[768,768]{1,0:T(8,128)} %get-tuple-element.5) | data formatting | bytes 4718592

commit v3 on v2

--- a/solution.py
+++ b/solution.py
@@ -48,7 +48,7 @@
 
 
 def kernel(trail, factor, lower, grad, top, out_rows, out_top, strail, s_high, s_low, f_all, zt, cx, zc, r_left, r_right, low, topv,
-           inv, inv_t, cmat, mmat, xmat, gbuf, p_hat, p_rows, planes, f_here, wst, r_a1, r_a2, a1, a2, r_b1, r_b2, b1, b2, r_c1, r_c2, c1, c2,
+           inv, i_high, i_low, t_high, t_low, cmat, m_high, m_low, xmat, gbuf, p_hat, p_rows, planes, f_here, wst, r_a1, r_a2, a1, a2, r_b1, r_b2, b1, b2, r_c1, r_c2, c1, c2,
            wfull, local_sem, send_sem, recv_sem):
     row, col = lax.axis_index("row"), lax.axis_index("col")
     y, x = lax.div(row, NX), lax.rem(row, NX)
@@ -213,14 +213,13 @@
         s_high[rows], s_low[rows] = split(strail[rows])
 
     forward("x", 0), forward("y", 0)
-    send("x", 2), send("y", 2), send("x", 4), send("y", 4)
+    send("x", 2), send("y", 2)
+    forward("x", 1), forward("y", 1)
+    send("x", 4), send("y", 4)
+    settle("x", 0), settle("y", 0)
+    send("x", 3), send("y", 3)
     local[3].wait()
     inverse_pair(low, inv, 0)
-    forward("x", 1), forward("y", 1)
-    settle("x", 0), settle("y", 0)
-    send("x", 3), send("y", 3)
-    inverse_pair(low, inv, 1)
-    forward("x", 2), forward("y", 2), forward("x", 4), forward("y", 4)
     grad_copy.wait_recv()
     cmat[:, 0:128] = gbuf[...].T
     for j in range(4):
@@ -228,17 +227,20 @@
         p_hat[rows] = cmat[rows, 0:128]
     settle("x", 1)
 
-    def multiply(j):
-        rows = pl.ds(aligned(lax.rem(y + j, NY), GROUP), GROUP)
-        f_high, f_low = split(f_all[rows])
+    def multiply(*groups):
+        parts = [split(f_all[pl.ds(aligned(lax.rem(y + j, NY), GROUP), GROUP)]) for j in groups]
+        high = jnp.concatenate([part[0] for part in parts], axis=0)
+        both = jnp.concatenate([part[0] for part in parts] + [part[1] for part in parts], axis=0)
+        size = GROUP * len(groups)
 
         @pl.loop(0, 4)
         def _(step):
             part = pl.ds(aligned(step, BLOCK), BLOCK)
             dims = ((1,), (1,))
-            zt[j, :, part] = (
-                contract(f_low, s_high[part], dims) + contract(f_high, s_low[part], dims) + contract(f_high, s_high[part], dims)
-            )
+            first = contract(both, s_high[part], dims)
+            value = first[:size] + first[size:] + contract(high, s_low[part], dims)
+            for i, j in enumerate(groups):
+                zt[j, :, part] = value[GROUP * i : GROUP * i + GROUP]
 
     crossing = {}
 
@@ -283,40 +285,41 @@
 
     multiply(0)
     cross(0)
-    forward("x", 3), forward("y", 3)
+    forward("x", 2), forward("y", 2), forward("x", 4), forward("y", 4)
     rearrange()
     begin(0)
+    forward("x", 3), forward("y", 3)
+    travel(0, 2)
     settle("x", 2), settle("x", 4)
-    multiply(1)
+    multiply(1, 3)
     cross(1)
-    travel(0, 2)
-    multiply(3)
     cross(3)
-    begin(1)
     travel(0, 3)
     for ring, item in (("y", 1), ("y", 2), ("y", 3), ("y", 4), ("x", 3)):
         settle(ring, item)
     multiply(2)
     cross(2)
+    travel(0, 4)
+    begin(1)
     begin(3)
-    travel(0, 4)
-    travel(1, 2)
     pass_on()
     begin(2)
+    travel(1, 2)
     travel(3, 2)
+    arrive(0)
+    travel(2, 2)
+    inverse_pair(low, inv, 1)
     travel(1, 3)
-    travel(2, 2)
-    arrive(0)
     travel(3, 3)
-    travel(1, 4)
     travel(2, 3)
     inverse_pair(low, inv, 2)
-    arrive(1)
+    travel(1, 4)
     travel(3, 4)
     travel(2, 4)
-    arrive(3)
     local[4].wait()
     start_gradient(low, topv, cmat)
+    arrive(1)
+    arrive(3)
     arrive(2)
     for copy in shares:
         copy.wait_recv()
@@ -354,10 +357,12 @@
     sa = scatter(lambda to: wst.at[rows_of(0, to * 128, 128)], 128, NX, at_x, x, r_a1)
     sb = scatter(lambda to: wst.at[rows_of(512, to * 128, 128)], 128, NY, at_y, y, r_b1)
     p_rows[...] = p_hat[...].T
+    inverse_blocks(low, inv)
     a1[...] = total(wst[rows_of(0, x * 128, 128)], sa, r_a1)
     sa = scatter(lambda to: a1.at[rows_of(0, to * 32, 32)], 32, NY, at_y, y, r_a2)
     b1[...] = total(wst[rows_of(512, y * 128, 128)], sb, r_b1)
     sb = scatter(lambda to: b1.at[rows_of(0, to * 32, 32)], 32, NX, at_x, x, r_b2)
+    inverse_halves(inv, i_high, i_low, t_high, t_low)
     a2[z] = total(a1[rows_of(0, y * 32, 32)], sa, r_a2)
     sa = gather(a2.at[z], NZ, at_z)
     b2[z] = total(b1[rows_of(0, x * 32, 32)], sb, r_b2)
@@ -366,8 +371,6 @@
     sc = scatter(lambda to: c1.at[rows_of(0, to * 16, 16)], 16, NX, at_x, x, r_c2)
     c2[y] = total(c1[rows_of(0, x * 16, 16)], sc, r_c2)
     sc = gather(c2.at[y], NY, at_y)
-    inverse_blocks(low, inv)
-    inverse_transposed(inv, inv_t)
     arrived(sc)
     rows = rows_of(1024, z * 64 + x * 16, 16)
     wfull[k, rows] = c2[0] + c2[1] + c2[2] + c2[3]
@@ -393,14 +396,14 @@
     sa = gather(wfull.at[k, rows_of(0, x * 128, 128)], NX, at_x)
     arrived(sb)
     sb = gather(wfull.at[k, rows_of(512, y * 128, 128)], NY, at_y)
-    out_rows[...] = dot6(p_rows[pl.ds(aligned(k, 64), 64)], inv[...])
     finals = []
     for start, copies in ((0, sa), (512, sb), (1024, sc)):
         arrived(copies)
         third = wfull.at[k, pl.ds(start, 512)]
         finals.append(push(third, third, partner))
+    out_rows[...] = dot6(p_rows[pl.ds(aligned(k, 64), 64)], inv[...])
     arrived(finals)
-    finish_gradient(inv, inv_t, cmat, wfull, mmat, xmat, out_top)
+    finish_gradient(i_high, i_low, t_high, t_low, cmat, wfull, m_high, m_low, xmat, out_top)
     for copy in pending:
         copy.wait_send()
 
@@ -453,11 +456,13 @@
     inv[two, 512:768] = jnp.zeros((BLOCK, BLOCK), F32)
 
 
-def inverse_transposed(inv, inv_t):
+def inverse_halves(inv, i_high, i_low, t_high, t_low):
     for i in range(3):
         for j in range(i, 3):
             rows, lanes = slice(BLOCK * i, BLOCK * i + BLOCK), slice(BLOCK * j, BLOCK * j + BLOCK)
-            inv_t[rows, lanes] = inv[lanes, rows].T
+            value = inv[lanes, rows]
+            i_high[lanes, rows], i_low[lanes, rows] = split(value)
+            t_high[rows, lanes], t_low[rows, lanes] = split(value.T)
 
 
 def start_gradient(low, topv, cmat):
@@ -476,7 +481,7 @@
             cmat[block, other] = value
 
 
-def finish_gradient(inv, inv_t, cmat, wfull, mmat, xmat, out_top):
+def finish_gradient(i_high, i_low, t_high, t_low, cmat, wfull, m_high, m_low, xmat, out_top):
     rows, lanes = iota((BLOCK, HALF), 0), iota((BLOCK, HALF), 1)
     for block in range(3):
         for side in range(2):
@@ -489,12 +494,23 @@
             if block < 2:
                 end = start + WIDTH - BLOCK * block
                 cmat[BLOCK * block + BLOCK :, column] -= wfull[side, start + BLOCK : end]
-    for i in range(3):
-        block = slice(BLOCK * i, BLOCK * i + BLOCK)
-        mmat[block] = dot3(inv_t[block, BLOCK * i :], cmat[BLOCK * i :])
+    def three(left_high, left_low, right_high, right_low):
+        dims = ((1,), (0,))
+        return (
+            contract(left_low, right_high, dims) + contract(left_high, right_low, dims) + contract(left_high, right_high, dims)
+        )
+
     for j in range(3):
-        block = slice(BLOCK * j, BLOCK * j + BLOCK)
-        xmat[:, block] = dot3(mmat[:, BLOCK * j :], inv[BLOCK * j :, block])
+        other = slice(BLOCK * j, BLOCK * j + BLOCK)
+        c_high, c_low = split(cmat[BLOCK * j :, other])
+        for i in range(3):
+            block, start = slice(BLOCK * i, BLOCK * i + BLOCK), BLOCK * max(i, j)
+            skip = start - BLOCK * j
+            value = three(t_high[block, start:], t_low[block, start:], c_high[skip:], c_low[skip:])
+            m_high[block, other], m_low[block, other] = split(value)
+    for j in range(3):
+        block, start = slice(BLOCK * j, BLOCK * j + BLOCK), BLOCK * j
+        xmat[:, block] = three(m_high[:, start:], m_low[:, start:], i_high[start:, block], i_low[start:, block])
     rows, lanes = iota((BLOCK, BLOCK), 0), iota((BLOCK, BLOCK), 1)
     for i in range(3):
         for j in range(3):
@@ -511,7 +527,7 @@
 def per_device(trail_grad, factor_rows, factor_top, rows_grad, top_grad):
     anywhere = pl.BlockSpec(memory_space=pl.ANY)
     inside = pl.BlockSpec(memory_space=pltpu.VMEM)
-    square = pltpu.VMEM((WIDTH, WIDTH), F32)
+    square, half_square = pltpu.VMEM((WIDTH, WIDTH), F32), pltpu.VMEM((WIDTH, WIDTH), BF16)
 
     def vmem(*shape):
         return pltpu.VMEM(shape, F32)
@@ -524,7 +540,7 @@
         scratch_shapes=[
             vmem(1024, 1024), pltpu.VMEM((1024, 1024), BF16), pltpu.VMEM((1024, 1024), BF16),
             vmem(WIDTH, 1024), vmem(4, GROUP, 1024), vmem(4, SUB, 1024), vmem(4, 8, SUB, 128), vmem(4, 4, SUB, 128),
-            vmem(4, 4, SUB, 128), square, square, square, square, square, square, square, vmem(128, WIDTH), vmem(WIDTH, 128),
+            vmem(4, 4, SUB, 128), square, square, square, *[half_square] * 4, square, half_square, half_square, square, vmem(128, WIDTH), vmem(WIDTH, 128),
             vmem(128, WIDTH), vmem(NZ, CHUNK, 128), vmem(WIDTH, 128), vmem(1536, 128), vmem(3, 128, 128), vmem(3, 32, 128), vmem(128, 128),
             vmem(8, 32, 128), vmem(3, 128, 128), vmem(3, 32, 128), vmem(128, 128), vmem(8, 32, 128), vmem(7, 64, 128),
             vmem(3, 16, 128), vmem(64, 128), vmem(4, 16, 128), vmem(2, 1536, 128), pltpu.SemaphoreType.DMA((8,)),

time: 100 us -> 100 us (level)
  no operation moved by 1% of the time
where the time goes in v3:
time: 100 us
  Pallas kernels  94.8 us (95%)
  local copies, waits for them, and re-layouts  4.84 us (5%)
    pallas_call x1, Pallas kernels, per_device(): pl.pallas_call(kernel, out_shape=(jax.ShapeDtypeStruct((64, WIDTH), F32),...  94.8 us
    unnamed x2, local copies, waits for them, and re-layouts  4.84 us

profile of v3, /device:TPU:1, one launch (start us, length us, event | category | flops | bytes accessed | tf_op | source)
XLA Modules:
  0.0 100.3 jit_solution(15777910656378398940)
XLA Ops:
  0.6 94.8 %shard_map.68 = (f32[64,768]{1,0:T(8,128)}, f32[768,768]{1,0:T(8,128)}) custom-call(f32[1024,1024]{1,0:T(8,128)} %trail.1, f32[48,1024]{1,0:T(8,128)} %bitcast.1, f32[768,768]{1,0:T(8,128)} %lower.1, f32[64,768]{1,0:T(8,128)} %grad.1, f32[768,768]{1,0:T(8,128)} %top.1), custom_call_target="tpu_custom_call" | custom-call | tf_op jit(solution)/shard_map/pallas_call | solution.py:535
  95.4 1.6 %copy.9 = f32[64,768]{1,0:T(8,128)} copy(f32[64,768]{1,0:T(8,128)} %get-tuple-element.4) | data formatting | bytes 393216
  97.0 3.2 %copy.10 = f32[768,768]{1,0:T(8,128)} copy(f32[768,768]{1,0:T(8,128)} %get-tuple-element.5) | data formatting | bytes 4718592

commit v4 on v3

--- a/solution.py
+++ b/solution.py
@@ -218,8 +218,6 @@
     send("x", 4), send("y", 4)
     settle("x", 0), settle("y", 0)
     send("x", 3), send("y", 3)
-    local[3].wait()
-    inverse_pair(low, inv, 0)
     grad_copy.wait_recv()
     cmat[:, 0:128] = gbuf[...].T
     for j in range(4):
@@ -286,9 +284,9 @@
     multiply(0)
     cross(0)
     forward("x", 2), forward("y", 2), forward("x", 4), forward("y", 4)
-    rearrange()
     begin(0)
     forward("x", 3), forward("y", 3)
+    rearrange()
     travel(0, 2)
     settle("x", 2), settle("x", 4)
     multiply(1, 3)
@@ -308,16 +306,14 @@
     travel(3, 2)
     arrive(0)
     travel(2, 2)
-    inverse_pair(low, inv, 1)
+    local[3].wait()
+    inverse_pair(low, inv, 0)
     travel(1, 3)
     travel(3, 3)
     travel(2, 3)
-    inverse_pair(low, inv, 2)
     travel(1, 4)
     travel(3, 4)
     travel(2, 4)
-    local[4].wait()
-    start_gradient(low, topv, cmat)
     arrive(1)
     arrive(3)
     arrive(2)
@@ -357,24 +353,29 @@
     sa = scatter(lambda to: wst.at[rows_of(0, to * 128, 128)], 128, NX, at_x, x, r_a1)
     sb = scatter(lambda to: wst.at[rows_of(512, to * 128, 128)], 128, NY, at_y, y, r_b1)
     p_rows[...] = p_hat[...].T
-    inverse_blocks(low, inv)
+    inverse_pair(low, inv, 1)
     a1[...] = total(wst[rows_of(0, x * 128, 128)], sa, r_a1)
     sa = scatter(lambda to: a1.at[rows_of(0, to * 32, 32)], 32, NY, at_y, y, r_a2)
     b1[...] = total(wst[rows_of(512, y * 128, 128)], sb, r_b1)
     sb = scatter(lambda to: b1.at[rows_of(0, to * 32, 32)], 32, NX, at_x, x, r_b2)
-    inverse_halves(inv, i_high, i_low, t_high, t_low)
+    inverse_pair(low, inv, 2)
     a2[z] = total(a1[rows_of(0, y * 32, 32)], sa, r_a2)
     sa = gather(a2.at[z], NZ, at_z)
     b2[z] = total(b1[rows_of(0, x * 32, 32)], sb, r_b2)
     sb = gather(b2.at[z], NZ, at_z)
     c1[...] = total(wst[rows_of(1024, z * 64, 64)], sc, r_c1)
     sc = scatter(lambda to: c1.at[rows_of(0, to * 16, 16)], 16, NX, at_x, x, r_c2)
+    inverse_blocks(low, inv)
     c2[y] = total(c1[rows_of(0, x * 16, 16)], sc, r_c2)
     sc = gather(c2.at[y], NY, at_y)
+    inverse_halves(inv, i_high, i_low, t_high, t_low)
+    local[4].wait()
+    start_gradient(low, topv, cmat)
     arrived(sc)
     rows = rows_of(1024, z * 64 + x * 16, 16)
     wfull[k, rows] = c2[0] + c2[1] + c2[2] + c2[3]
     sc = gather(wfull.at[k, rows], NX, at_x)
+    out_rows[...] = dot6(p_rows[pl.ds(aligned(k, 64), 64)], inv[...])
 
     def over_z(ref):
         value = ref[0]
@@ -397,11 +398,21 @@
     arrived(sb)
     sb = gather(wfull.at[k, rows_of(512, y * 128, 128)], NY, at_y)
     finals = []
-    for start, copies in ((0, sa), (512, sb), (1024, sc)):
-        arrived(copies)
-        third = wfull.at[k, pl.ds(start, 512)]
-        finals.append(push(third, third, partner))
-    out_rows[...] = dot6(p_rows[pl.ds(aligned(k, 64), 64)], inv[...])
+
+    def hand_over(base, size, extent, me, copies):
+        def give(owner):
+            block = wfull.at[k, rows_of(base, owner * size, size)]
+            finals.append(push(block, block, partner))
+
+        give(me)
+        order = sorted(range(1, extent), key=lambda d: min(d, extent - d))
+        for d in order:
+            copies[d - 1].wait_recv()
+            give(lax.rem(me - d + extent, extent))
+
+    hand_over(0, 128, NX, x, sa)
+    hand_over(512, 128, NY, y, sb)
+    hand_over(1024, 64, NZ, z, sc)
     arrived(finals)
     finish_gradient(i_high, i_low, t_high, t_low, cmat, wfull, m_high, m_low, xmat, out_top)
     for copy in pending:

time: 100 us -> 98.4 us (0.984)
  Pallas kernels: 94.8 us -> 92.8 us
    pallas_call x1, Pallas kernels: 94.8 us -> 92.8 us  [per_device(): pl.pallas_call(kernel, out_shape=(jax.ShapeDtypeStruct((64, WIDTH), F32),...]
where the time goes in v4:
time: 98.4 us; the launch traced here: 98.3 us
  Pallas kernels  92.8 us (94%)
  local copies, waits for them, and re-layouts  4.84 us (5%)
    pallas_call x1, Pallas kernels, per_device(): pl.pallas_call(kernel, out_shape=(jax.ShapeDtypeStruct((64, WIDTH), F32),...  92.8 us
    unnamed x2, local copies, waits for them, and re-layouts  4.84 us

profile of v4, /device:TPU:1, one launch (start us, length us, event | category | flops | bytes accessed | tf_op | source)
XLA Modules:
  0.0 98.3 jit_solution(16551228754195259823)
XLA Ops:
  0.6 92.8 %shard_map.68 = (f32[64,768]{1,0:T(8,128)}, f32[768,768]{1,0:T(8,128)}) custom-call(f32[1024,1024]{1,0:T(8,128)} %trail.1, f32[48,1024]{1,0:T(8,128)} %bitcast.1, f32[768,768]{1,0:T(8,128)} %lower.1, f32[64,768]{1,0:T(8,128)} %grad.1, f32[768,768]{1,0:T(8,128)} %top.1), custom_call_target="tpu_custom_call" | custom-call | tf_op jit(solution)/shard_map/pallas_call | solution.py:546
  93.5 1.6 %copy.9 = f32[64,768]{1,0:T(8,128)} copy(f32[64,768]{1,0:T(8,128)} %get-tuple-element.4) | data formatting | bytes 393216
  95.1 3.2 %copy.10 = f32[768,768]{1,0:T(8,128)} copy(f32[768,768]{1,0:T(8,128)} %get-tuple-element.5) | data formatting | bytes 4718592

commit v5 on v4

--- a/solution.py
+++ b/solution.py
@@ -49,7 +49,7 @@
 
 def kernel(trail, factor, lower, grad, top, out_rows, out_top, strail, s_high, s_low, f_all, zt, cx, zc, r_left, r_right, low, topv,
            inv, i_high, i_low, t_high, t_low, cmat, m_high, m_low, xmat, gbuf, p_hat, p_rows, planes, f_here, wst, r_a1, r_a2, a1, a2, r_b1, r_b2, b1, b2, r_c1, r_c2, c1, c2,
-           wfull, local_sem, send_sem, recv_sem):
+           wfull, rows_v, top_v, local_sem, send_sem, recv_sem):
     row, col = lax.axis_index("row"), lax.axis_index("col")
     y, x = lax.div(row, NX), lax.rem(row, NX)
     z, k = lax.div(col, 2), lax.rem(col, 2)
@@ -375,7 +375,9 @@
     rows = rows_of(1024, z * 64 + x * 16, 16)
     wfull[k, rows] = c2[0] + c2[1] + c2[2] + c2[3]
     sc = gather(wfull.at[k, rows], NX, at_x)
-    out_rows[...] = dot6(p_rows[pl.ds(aligned(k, 64), 64)], inv[...])
+    rows_v[...] = dot6(p_rows[pl.ds(aligned(k, 64), 64)], inv[...])
+    written = [pltpu.make_async_copy(rows_v, out_rows, local_sem.at[7])]
+    written[0].start()
 
     def over_z(ref):
         value = ref[0]
@@ -414,7 +416,9 @@
     hand_over(512, 128, NY, y, sb)
     hand_over(1024, 64, NZ, z, sc)
     arrived(finals)
-    finish_gradient(i_high, i_low, t_high, t_low, cmat, wfull, m_high, m_low, xmat, out_top)
+    finish_gradient(i_high, i_low, t_high, t_low, cmat, wfull, m_high, m_low, xmat, top_v, out_top, local_sem, written)
+    for copy in written:
+        copy.wait()
     for copy in pending:
         copy.wait_send()
 
@@ -492,7 +496,7 @@
             cmat[block, other] = value
 
 
-def finish_gradient(i_high, i_low, t_high, t_low, cmat, wfull, m_high, m_low, xmat, out_top):
+def finish_gradient(i_high, i_low, t_high, t_low, cmat, wfull, m_high, m_low, xmat, top_v, out_top, local_sem, written):
     rows, lanes = iota((BLOCK, HALF), 0), iota((BLOCK, HALF), 1)
     for block in range(3):
         for side in range(2):
@@ -527,38 +531,64 @@
         for j in range(3):
             block, other = slice(BLOCK * i, BLOCK * i + BLOCK), slice(BLOCK * j, BLOCK * j + BLOCK)
             if j > i:
-                out_top[block, other] = jnp.zeros((BLOCK, BLOCK), F32)
+                top_v[block, other] = jnp.zeros((BLOCK, BLOCK), F32)
                 continue
             value = xmat[block, other] + xmat[other, block].T
             if i == j:
                 value = jnp.where(rows > lanes, value, jnp.where(rows == lanes, 0.5 * value, 0.0))
-            out_top[block, other] = value
+            top_v[block, other] = value
+        copy = pltpu.make_async_copy(top_v.at[block], out_top.at[block], local_sem.at[8 + i])
+        copy.start()
+        written.append(copy)
+
+
+def deliver(rows_in, top_in, rows_out, top_out, rows_v, top_v, in_sem, out_sem):
+    parts = [(rows_in, rows_v, rows_out)]
+    for i in range(6):
+        span = pl.ds(HALF * i, HALF)
+        parts.append((top_in.at[span], top_v.at[span], top_out.at[span]))
+    incoming = [pltpu.make_async_copy(part[0], part[1], in_sem.at[i]) for i, part in enumerate(parts)]
+    outgoing = [pltpu.make_async_copy(part[1], part[2], out_sem.at[i]) for i, part in enumerate(parts)]
+    for copy in incoming:
+        copy.start()
+    for before, after in zip(incoming, outgoing):
+        before.wait()
+        after.start()
+    for copy in outgoing:
+        copy.wait()
 
 
 def per_device(trail_grad, factor_rows, factor_top, rows_grad, top_grad):
     anywhere = pl.BlockSpec(memory_space=pl.ANY)
-    inside = pl.BlockSpec(memory_space=pltpu.VMEM)
     square, half_square = pltpu.VMEM((WIDTH, WIDTH), F32), pltpu.VMEM((WIDTH, WIDTH), BF16)
 
     def vmem(*shape):
         return pltpu.VMEM(shape, F32)
 
-    return pl.pallas_call(
+    shapes = (jax.ShapeDtypeStruct((64, WIDTH), F32), jax.ShapeDtypeStruct((WIDTH, WIDTH), F32))
+    results = pl.pallas_call(
         kernel,
-        out_shape=(jax.ShapeDtypeStruct((64, WIDTH), F32), jax.ShapeDtypeStruct((WIDTH, WIDTH), F32)),
+        out_shape=shapes,
         in_specs=[anywhere] * 5,
-        out_specs=(inside, inside),
+        out_specs=(anywhere, anywhere),
         scratch_shapes=[
             vmem(1024, 1024), pltpu.VMEM((1024, 1024), BF16), pltpu.VMEM((1024, 1024), BF16),
             vmem(WIDTH, 1024), vmem(4, GROUP, 1024), vmem(4, SUB, 1024), vmem(4, 8, SUB, 128), vmem(4, 4, SUB, 128),
             vmem(4, 4, SUB, 128), square, square, square, *[half_square] * 4, square, half_square, half_square, square, vmem(128, WIDTH), vmem(WIDTH, 128),
             vmem(128, WIDTH), vmem(NZ, CHUNK, 128), vmem(WIDTH, 128), vmem(1536, 128), vmem(3, 128, 128), vmem(3, 32, 128), vmem(128, 128),
             vmem(8, 32, 128), vmem(3, 128, 128), vmem(3, 32, 128), vmem(128, 128), vmem(8, 32, 128), vmem(7, 64, 128),
-            vmem(3, 16, 128), vmem(64, 128), vmem(4, 16, 128), vmem(2, 1536, 128), pltpu.SemaphoreType.DMA((8,)),
+            vmem(3, 16, 128), vmem(64, 128), vmem(4, 16, 128), vmem(2, 1536, 128), vmem(64, WIDTH), square, pltpu.SemaphoreType.DMA((11,)),
             pltpu.SemaphoreType.DMA((SEMAPHORES,)), pltpu.SemaphoreType.DMA((SEMAPHORES,)),
         ],
         compiler_params=pltpu.CompilerParams(collective_id=0, has_side_effects=True, vmem_limit_bytes=62 << 20),
     )(trail_grad, factor_rows.T, factor_top, rows_grad, top_grad)
+    return pl.pallas_call(
+        deliver,
+        out_shape=shapes,
+        in_specs=[anywhere] * 2,
+        out_specs=(anywhere, anywhere),
+        scratch_shapes=[vmem(64, WIDTH), square, pltpu.SemaphoreType.DMA((7,)), pltpu.SemaphoreType.DMA((7,))],
+    )(*results)
 
 
 def solution(mesh):

time: 98.4 us -> 96.3 us (0.979)
  local copies, waits for them, and re-layouts: 4.84 us -> 0 us
  Pallas kernels: 92.8 us -> 95.3 us
    unnamed x2 -> x0, local copies, waits for them, and re-layouts: 4.84 us -> none
    pallas_call x1 -> x2, Pallas kernels: 92.8 us -> 95.3 us  [the longest x1 92.7 us: per_device(): pl.pallas_call(kernel, out_shape=shapes, in_specs=[anywhere] * 5, out_spe...]
where the time goes in v5:
time: 96.3 us; the launch traced here: 96.2 us
  Pallas kernels  95.3 us (99%)
    pallas_call x1, Pallas kernels, per_device(): pl.pallas_call(kernel, out_shape=shapes, in_specs=[anywhere] * 5, out_spe...  92.7 us
    pallas_call x1, Pallas kernels, per_device(): pl.pallas_call(deliver, out_shape=shapes, in_specs=[anywhere] * 2, out_sp...  2.61 us

profile of v5, /device:TPU:1, one launch (start us, length us, event | category | flops | bytes accessed | tf_op | source)
XLA Modules:
  0.0 96.2 jit_solution(9336828768437529769)
XLA Ops:
  0.6 92.7 %shard_map.68 = (f32[64,768]{1,0:T(8,128)}, f32[768,768]{1,0:T(8,128)}) custom-call(f32[1024,1024]{1,0:T(8,128)} %trail.1, f32[48,1024]{1,0:T(8,128)} %bitcast.1, f32[768,768]{1,0:T(8,128)} %lower.1, f32[64,768]{1,0:T(8,128)} %grad.1, f32[768,768]{1,0:T(8,128)} %top.1), custom_call_target="tpu_custom_call" | custom-call | tf_op jit(solution)/shard_map/pallas_call | solution.py:569
  93.4 2.6 %shard_map.69 = (f32[64,768]{1,0:T(8,128)}, f32[768,768]{1,0:T(8,128)}) custom-call(f32[64,768]{1,0:T(8,128)} %get-tuple-element.4.rows_in, f32[768,768]{1,0:T(8,128)} %get-tuple-element.5.top_in), custom_call_target="tpu_custom_call" | custom-call | tf_op jit(solution)/shard_map/pallas_call | solution.py:585

commit v6 on v5

--- a/solution.py
+++ b/solution.py
@@ -295,11 +295,11 @@
     travel(0, 3)
     for ring, item in (("y", 1), ("y", 2), ("y", 3), ("y", 4), ("x", 3)):
         settle(ring, item)
+    begin(1)
+    begin(3)
     multiply(2)
     cross(2)
     travel(0, 4)
-    begin(1)
-    begin(3)
     pass_on()
     begin(2)
     travel(1, 2)

time: 96.3 us -> 97 us (level)
  no operation moved by 1% of the time
where the time goes in v6:
time: 97 us; the launch traced here: 96.9 us
  Pallas kernels  96.1 us (99%)
    pallas_call x1, Pallas kernels, per_device(): pl.pallas_call(kernel, out_shape=shapes, in_specs=[anywhere] * 5, out_spe...  93.5 us
    pallas_call x1, Pallas kernels, per_device(): pl.pallas_call(deliver, out_shape=shapes, in_specs=[anywhere] * 2, out_sp...  2.61 us

profile of v6, /device:TPU:1, one launch (start us, length us, event | category | flops | bytes accessed | tf_op | source)
XLA Modules:
  0.0 96.9 jit_solution(9482373916836807290)
XLA Ops:
  0.6 93.5 %shard_map.68 = (f32[64,768]{1,0:T(8,128)}, f32[768,768]{1,0:T(8,128)}) custom-call(f32[1024,1024]{1,0:T(8,128)} %trail.1, f32[48,1024]{1,0:T(8,128)} %bitcast.1, f32[768,768]{1,0:T(8,128)} %lower.1, f32[64,768]{1,0:T(8,128)} %grad.1, f32[768,768]{1,0:T(8,128)} %top.1), custom_call_target="tpu_custom_call" | custom-call | tf_op jit(solution)/shard_map/pallas_call | solution.py:569
  94.1 2.6 %shard_map.69 = (f32[64,768]{1,0:T(8,128)}, f32[768,768]{1,0:T(8,128)}) custom-call(f32[64,768]{1,0:T(8,128)} %get-tuple-element.4.rows_in, f32[768,768]{1,0:T(8,128)} %get-tuple-element.5.top_in), custom_call_target="tpu_custom_call" | custom-call | tf_op jit(solution)/shard_map/pallas_call | solution.py:585
